TPU v7x, 32 devices: a whole 2x2x4 slice. The times are simulated.
32 devices in a mesh: branch: 2 (over x), dp: 16 (over z, y, core).
Axes of the slice: x: 2, y: 2, z: 4, core: 2. Of those that a mesh axis runs over, the one named last changes fastest.
Arguments:
- inputs: bfloat16 [96, 816, 512], P('dp'), may hold values from -6 to 6
- window_count: int32 [16], P('dp'), may hold values from 1 to 6, as said below
- branch_blocks: bfloat16 [2, 2, 23552, 512], P('branch', None, 'dp')
- branch_gains: float32 [2, 512], P('branch'), may hold values from 0.1 to 1.9
- branch_biases: float32 [2, 4, 512], P('branch'), may hold values from -2.5 to 2.5
- merge_weight: bfloat16 [1024, 512], replicated, may hold values from -0.1875 to 0.1875
- ff_in: bfloat16 [512, 2048], replicated, may hold values from -0.25 to 0.25
- ff_in_bias: float32 [2048], replicated, may hold values from -2.5 to 2.5
- ff_out: bfloat16 [2048, 512], replicated, may hold values from -0.25 to 0.25
- shared_biases: float32 [4, 512], replicated, may hold values from -2.5 to 2.5
- shared_gains: float32 [2, 512], replicated, may hold values from 0.1 to 1.9
- d_out: bfloat16 [48, 2, 1, 816, 512], P('dp', 'branch'), may hold values from -6 to 6
Outputs:
- layer_out: bfloat16 [48, 2, 1, 816, 512], P('dp', 'branch')
- grad_inputs: bfloat16 [48, 2, 1, 816, 512], P('dp', 'branch')
- grad_branch_blocks: float32 [2, 2, 23552, 512], P('branch', None, 'dp')
- grad_branch_gains: float32 [2, 512], P('branch')
- grad_branch_biases: float32 [2, 4, 512], P('branch')
- grad_merge_weight: float32 [1024, 512], replicated
- grad_ff_in: float32 [512, 2048], replicated
- grad_ff_in_bias: float32 [2048], replicated
- grad_ff_out: float32 [2048, 512], replicated
- grad_shared_biases: float32 [4, 512], replicated
- grad_shared_gains: float32 [2, 512], replicated
Inputs may be any that keep to these rules, and one draw needn't show every extreme that they name: window_count[j] is the number of live windows among windows j * 6 to (j + 1) * 6 - 1, the live ones first; at least one entry equals 6.
All inputs are finite; a program needn't handle non-finite values.
Results may differ from a plain program's by a relative error of at most 0.015.
Values may be sent and summed in bfloat16 or wider, within the bound.
A program may use at most 512 MiB of HBM per device.

v0:
```python
from functools import partial
import jax
import jax.numpy as jnp
from jax import lax
from jax.sharding import PartitionSpec as P

SCALE_A = 12
SCALE_B = 16
MICRO = 3
GRAD_GROUPS = 2
BLOCKS = 92
EPSILON = 1e-05


def layer_norm(values, norm_gain, norm_shift):
    centre = values - jnp.mean(values, axis=-1, keepdims=True)
    spread = jnp.mean(centre * centre, axis=-1, keepdims=True)
    return centre * lax.rsqrt(spread + EPSILON) * norm_gain + norm_shift


def gelu_exact(values):
    return jax.nn.gelu(values, approximate=False)


def column_sum(values):
    return jnp.sum(values.astype(jnp.float32), axis=(0, 1))


def pad_taps(values, tap_total):
    return jnp.pad(values, ((0, 0), (0, tap_total - values.shape[1]), (0, 0)))


def past_windows(values, tap_count, begin, finish):
    batch_size, length, channels = values.shape
    padded = jnp.concatenate(
        [jnp.zeros((batch_size, tap_count - 1, channels), values.dtype), values], axis=1
    )
    offsets = jnp.arange(length)[:, None] + jnp.arange(begin, finish)[None, :]
    return padded[:, offsets, :]


def future_windows(values, tap_count):
    batch_size, length, channels = values.shape
    padded = jnp.concatenate(
        [values, jnp.zeros((batch_size, tap_count - 1, channels), values.dtype)], axis=1
    )
    offsets = jnp.arange(length)[:, None] + (tap_count - 1) - jnp.arange(tap_count)[None, :]
    return padded[:, offsets, :]


def split_blocks(blocks, stride, tap_count):
    return (
        blocks[:stride],
        blocks[stride : stride + tap_count],
        blocks[stride + tap_count : 2 * stride + tap_count],
    )


def branch_forward(stride, tap_total, values, blocks, norm_gain, biases):
    batch_size, length, channels = values.shape
    tap_count = length // stride
    down_weight, iso_weight, up_weight = split_blocks(blocks, stride, tap_count)
    tap_rows = values.reshape(batch_size, tap_count, stride, channels)
    act_full = jnp.tanh(
        jnp.einsum("btrd,rdo->bto", tap_rows, down_weight, preferred_element_type=jnp.float32)
        + biases[0]
    )
    windows = past_windows(act_full.astype(jnp.bfloat16), tap_count, 0, tap_count)
    iso_full = jnp.tanh(
        jnp.einsum("btsd,sdo->bto", windows, iso_weight, preferred_element_type=jnp.float32)
        + biases[1]
    )
    expanded = jnp.einsum(
        "bte,red->btrd",
        iso_full.astype(jnp.bfloat16),
        up_weight,
        preferred_element_type=jnp.float32,
    )
    residual = (
        expanded.reshape(batch_size, length, channels) + biases[2] + values.astype(jnp.float32)
    )
    branch_out = layer_norm(residual, norm_gain, biases[3])
    return (branch_out, residual, pad_taps(act_full, tap_total), pad_taps(iso_full, tap_total))


def branch_backward(
    stride, tap_total, values, grad_branch, residual, act_full, iso_full, blocks, norm_gain, biases
):
    batch_size, length, channels = values.shape
    tap_count = length // stride
    down_weight, iso_weight, up_weight = split_blocks(blocks, stride, tap_count)
    act_used = act_full[:, :tap_count]
    iso_used = iso_full[:, :tap_count]
    unused, norm_back = jax.vjp(layer_norm, residual, norm_gain, biases[3])
    grad_residual, grad_gain, grad_shift = norm_back(grad_branch.astype(jnp.float32))
    grad_expanded = grad_residual.astype(jnp.bfloat16)
    grad_taps = grad_expanded.reshape(batch_size, tap_count, stride, channels)
    grad_iso_out = jnp.einsum(
        "btrd,red->bte", grad_taps, up_weight, preferred_element_type=jnp.float32
    )
    grad_iso = (grad_iso_out * (1.0 - iso_used * iso_used)).astype(jnp.bfloat16)
    grad_act = jnp.einsum(
        "btso,sdo->btd",
        future_windows(grad_iso, tap_count),
        iso_weight,
        preferred_element_type=jnp.float32,
    )
    grad_down = (grad_act * (1.0 - act_used * act_used)).astype(jnp.bfloat16)
    grad_rows = jnp.einsum(
        "bto,rdo->btrd", grad_down, down_weight, preferred_element_type=jnp.float32
    )
    grad_values = grad_residual + grad_rows.reshape(batch_size, length, channels)
    vectors = jnp.stack(
        [
            grad_gain,
            column_sum(grad_down),
            column_sum(grad_iso),
            column_sum(grad_expanded),
            grad_shift,
        ]
    )
    return (
        grad_values,
        vectors,
        pad_taps(grad_down, tap_total),
        pad_taps(grad_iso, tap_total),
        grad_expanded,
    )


def group_grads(
    group_index, stride, values, activation, isometric, grad_down, grad_iso, grad_expanded
):
    batch_size, length, channels = values.shape
    tap_count = length // stride
    per_group = BLOCKS // GRAD_GROUPS
    first_block = group_index * per_group
    end_block = first_block + per_group
    pieces = []
    covered = 0
    begin, finish = (max(first_block, 0), min(end_block, stride))
    if begin < finish:
        tap_rows = values.reshape(batch_size, tap_count, stride, channels)
        pieces.append(
            jnp.einsum(
                "btrd,bto->rdo",
                tap_rows,
                grad_down[:, :tap_count],
                preferred_element_type=jnp.float32,
            )
        )
        covered += finish - begin
    begin, finish = (max(first_block, stride), min(end_block, stride + tap_count))
    windows = past_windows(activation[:, :tap_count], tap_count, begin - stride, finish - stride)
    pieces.append(
        jnp.einsum(
            "btsd,bto->sdo", windows, grad_iso[:, :tap_count], preferred_element_type=jnp.float32
        )
    )
    covered += finish - begin
    begin, finish = (max(first_block, stride + tap_count), min(end_block, 2 * stride + tap_count))
    if begin < finish:
        grad_taps = grad_expanded.reshape(batch_size, tap_count, stride, channels)
        pieces.append(
            jnp.einsum(
                "bte,btrd->red",
                isometric[:, :tap_count],
                grad_taps,
                preferred_element_type=jnp.float32,
            )
        )
        covered += finish - begin
    if covered < per_group:
        pieces.append(jnp.zeros((per_group - covered, channels, channels), jnp.float32))
    return jnp.concatenate(pieces, axis=0).reshape(per_group * channels, channels)


def group_term(
    group_index, branch_index, values, activation, isometric, grad_down, grad_iso, grad_expanded
):
    return lax.cond(
        branch_index == 0,
        partial(group_grads, group_index, SCALE_A),
        partial(group_grads, group_index, SCALE_B),
        values,
        activation,
        isometric,
        grad_down,
        grad_iso,
        grad_expanded,
    )


def per_device(
    inputs,
    window_count,
    branch_blocks,
    branch_gains,
    branch_biases,
    merge_weight,
    ff_in,
    ff_in_bias,
    ff_out,
    shared_biases,
    shared_gains,
    d_out,
):
    branch_index = lax.axis_index("branch")
    slot_total, length, channels = inputs.shape
    per_micro = slot_total // MICRO
    half_micro = per_micro // 2
    tap_total = max(length // SCALE_A, length // SCALE_B)
    gathered = lax.all_gather(branch_blocks, "dp", axis=2, tiled=True)
    blocks = gathered.reshape(-1, channels, channels)
    norm_gain = branch_gains[0]
    biases = branch_biases[0]
    live_count = window_count[0]
    forward_pair = (
        partial(branch_forward, SCALE_A, tap_total),
        partial(branch_forward, SCALE_B, tap_total),
    )
    backward_pair = (
        partial(branch_backward, SCALE_A, tap_total),
        partial(branch_backward, SCALE_B, tap_total),
    )
    shared_totals = [
        jnp.zeros(merge_weight.shape, jnp.float32),
        jnp.zeros(ff_in.shape, jnp.float32),
        jnp.zeros(ff_in_bias.shape, jnp.float32),
        jnp.zeros(ff_out.shape, jnp.float32),
        jnp.zeros(shared_biases.shape, jnp.float32),
        jnp.zeros(shared_gains.shape, jnp.float32),
    ]
    vector_total = jnp.zeros((5, channels), jnp.float32)
    kept_parts = []
    outputs = []
    input_parts = []
    for micro_index in range(MICRO):
        start = micro_index * per_micro
        values = inputs[start : start + per_micro]
        branch_out, residual, act_full, iso_full = lax.cond(
            branch_index == 0, forward_pair[0], forward_pair[1], values, blocks, norm_gain, biases
        )
        joined = lax.all_to_all(
            branch_out.astype(jnp.bfloat16), "branch", split_axis=0, concat_axis=2, tiled=True
        )
        merged = (
            jnp.einsum("btk,ko->bto", joined, merge_weight, preferred_element_type=jnp.float32)
            + shared_biases[0]
        )
        normed_full, norm_one_back = jax.vjp(layer_norm, merged, shared_gains[0], shared_biases[1])
        normed = normed_full.astype(jnp.bfloat16)
        inner_pre = (
            jnp.einsum("btd,df->btf", normed, ff_in, preferred_element_type=jnp.float32)
            + ff_in_bias
        )
        hidden_full, gelu_back = jax.vjp(gelu_exact, inner_pre)
        hidden = hidden_full.astype(jnp.bfloat16)
        outer_pre = (
            jnp.einsum("btf,fd->btd", hidden, ff_out, preferred_element_type=jnp.float32)
            + shared_biases[2]
        )
        result, norm_two_back = jax.vjp(
            layer_norm, merged + outer_pre, shared_gains[1], shared_biases[3]
        )
        window_ids = start + branch_index * half_micro + jnp.arange(half_micro)
        alive_mask = (window_ids < live_count).astype(jnp.float32)[:, None, None]
        outputs.append((result * alive_mask).astype(jnp.bfloat16))
        cotangent = d_out[micro_index, 0].astype(jnp.float32) * alive_mask
        grad_sum, grad_gain_two, grad_shift_two = norm_two_back(cotangent)
        grad_outer = grad_sum.astype(jnp.bfloat16)
        grad_hidden = jnp.einsum(
            "btd,fd->btf", grad_outer, ff_out, preferred_element_type=jnp.float32
        )
        grad_inner = gelu_back(grad_hidden)[0].astype(jnp.bfloat16)
        grad_normed = jnp.einsum(
            "btf,df->btd", grad_inner, ff_in, preferred_element_type=jnp.float32
        )
        grad_norm_in, grad_gain_one, grad_shift_one = norm_one_back(grad_normed)
        grad_merged = (grad_sum + grad_norm_in).astype(jnp.bfloat16)
        grad_joined = jnp.einsum(
            "bto,ko->btk", grad_merged, merge_weight, preferred_element_type=jnp.float32
        ).astype(jnp.bfloat16)
        terms = (
            jnp.einsum("btk,bto->ko", joined, grad_merged, preferred_element_type=jnp.float32),
            jnp.einsum("btd,btf->df", normed, grad_inner, preferred_element_type=jnp.float32),
            column_sum(grad_inner),
            jnp.einsum("btf,btd->fd", hidden, grad_outer, preferred_element_type=jnp.float32),
            jnp.stack(
                [column_sum(grad_merged), grad_shift_one, column_sum(grad_outer), grad_shift_two]
            ),
            jnp.stack([grad_gain_one, grad_gain_two]),
        )
        shared_totals = [running + addend for running, addend in zip(shared_totals, terms)]
        grad_branch = lax.all_to_all(grad_joined, "branch", split_axis=2, concat_axis=0, tiled=True)
        grad_values, vectors, grad_down, grad_iso, grad_expanded = lax.cond(
            branch_index == 0,
            backward_pair[0],
            backward_pair[1],
            values,
            grad_branch,
            residual,
            act_full,
            iso_full,
            blocks,
            norm_gain,
            biases,
        )
        vector_total = vector_total + vectors
        summed_values = lax.psum_scatter(
            grad_values.astype(jnp.bfloat16), "branch", scatter_dimension=0, tiled=True
        )
        input_parts.append(summed_values)
        activation = act_full.astype(jnp.bfloat16)
        isometric = iso_full.astype(jnp.bfloat16)
        kept_parts.append((activation, isometric, grad_down, grad_iso, grad_expanded))
    activation_all = jnp.concatenate([entry[0] for entry in kept_parts], axis=0)
    isometric_all = jnp.concatenate([entry[1] for entry in kept_parts], axis=0)
    grad_down_all = jnp.concatenate([entry[2] for entry in kept_parts], axis=0)
    grad_iso_all = jnp.concatenate([entry[3] for entry in kept_parts], axis=0)
    grad_expanded_all = jnp.concatenate([entry[4] for entry in kept_parts], axis=0)
    block_result = []
    for group_index in range(GRAD_GROUPS):
        term = group_term(
            group_index,
            branch_index,
            inputs,
            activation_all,
            isometric_all,
            grad_down_all,
            grad_iso_all,
            grad_expanded_all,
        )
        block_result.append(lax.psum_scatter(term, "dp", scatter_dimension=0, tiled=True))
    vector_full = jnp.where((jnp.arange(2) == branch_index)[:, None, None], vector_total[None], 0.0)
    summed = lax.psum(
        (
            shared_totals[0],
            shared_totals[1],
            shared_totals[2],
            shared_totals[3],
            shared_totals[4],
            shared_totals[5],
            vector_full,
        ),
        ("branch", "dp"),
    )
    own_vectors = lax.dynamic_slice_in_dim(summed[6], branch_index, 1, 0)
    layer_out = jnp.stack(outputs)[:, None]
    grad_inputs = jnp.stack(input_parts)[:, None]
    grad_blocks = jnp.stack(block_result)[None]
    return (
        layer_out,
        grad_inputs,
        grad_blocks,
        own_vectors[:, 0],
        own_vectors[:, 1:],
        summed[0],
        summed[1],
        summed[2],
        summed[3],
        summed[4],
        summed[5],
    )


def solution(mesh):
    placed = (
        P("dp", None, None),
        P("dp"),
        P("branch", None, "dp", None),
        P("branch", None),
        P("branch", None, None),
        P(),
        P(),
        P(),
        P(),
        P(),
        P(),
        P("dp", "branch", None, None, None),
    )
    return jax.shard_map(
        per_device,
        mesh=mesh,
        in_specs=placed,
        out_specs=(
            P("dp", "branch", None, None, None),
            P("dp", "branch", None, None, None),
            P("branch", None, "dp", None),
            P("branch", None),
            P("branch", None, None),
            P(),
            P(),
            P(),
            P(),
            P(),
            P(),
        ),
        check_vma=False,
    )
```

profile of v0, /device:TPU:0, one launch (start us, length us, event | category | flops | bytes accessed | tf_op | source)
XLA Modules:
  0.0 2379.5 jit_solution(8030178385065969234)
XLA Ops:
  15.6 233.9 %all-gather.2.cloned.1.call-done = bf16[1,2,23552,512]{3,2,1,0:T(8,128)(2,1)} async-done(((bf16[1,2,1472,512]{3,2,1,0:T(8,128)(2,1)}), bf16[1,2,23552,512]{3,2,1,0:T(8,128)(2,1)}) %all-gather.2.cloned.1.call-update) | async-done | bytes 48234512 | tf_op jit(solution)/shard_map/all_gather | solution.py:213
  249.5 94.2 %conditional.10 = (bf16[2,816,512]{2,1,0:T(8,128)(2,1)}, f32[2,816,512]{2,1,0:T(8,128)}, f32[2,68,512]{2,1,0:T(8,128)S(1)}, f32[2,68,512]{2,1,0:T(8,128)}) conditional(s32[]{:T(128)} %convert_element_type.450, (bf16[2,816,512]{2,0,1:T(2,128)(2,1)}, bf16[92,512,512]{2,1,0:T(8,128)(2,1)}, f32[4,512]{1,0:T(4,128)S(1)}, ...), branch_computations={%region_20.0_spmd, %region_23.0_spmd} | conditional | flops 6570222080 | bytes 131432216 | solution.py:241
  262.0 27.4 %gather_fusion.9 = bf16[4624,2,512]{2,1,0:T(2,128)(2,1)} fusion(bf16[2,135,512]{2,0,1:T(2,128)(2,1)S(1)} %concatenate.55.clone, s32[5120]{0:T(1024)S(1)} %pad_clamp_fusion.5), kind=kCustom, calls=%fused_computation.5 | custom fusion | bytes 18958400 | tf_op jit(solution)/shard_map/cond/branch_1_fun/gather | solution.py:39
  289.4 33.7 %fusion.251 = f32[2,68,512]{2,1,0:T(8,128)S(1)} fusion(bf16[92,512,512]{2,1,0:T(8,128)(2,1)} %get-tuple-element.277, bf16[2,68,68,512]{3,0,2,1:T(2,128)(2,1)} %bitcast.970, f32[512]{0:T(512)S(1)} %bitcast.1114), kind=kOutput, calls=%fused_computation.171 | convolution fusion | flops 4848685056 | bytes 45402112 | tf_op jit(solution)/shard_map/cond/branch_1_fun/btsd,sdo->bto/dot_general | solution.py:70
  352.8 87.1 %conditional.9 = (bf16[2,816,512]{2,1,0:T(8,128)(2,1)}, f32[2,816,512]{2,1,0:T(8,128)}, f32[2,68,512]{2,1,0:T(8,128)S(1)}, f32[2,68,512]{2,1,0:T(8,128)}) conditional(s32[]{:T(128)} %convert_element_type.450, (bf16[2,816,512]{2,0,1:T(2,128)(2,1)}, bf16[92,512,512]{2,1,0:T(8,128)(2,1)}, f32[4,512]{1,0:T(4,128)S(1)}, ...), branch_computations={%region_10.0_spmd, %region_13.0_spmd} | conditional | flops 6570222080 | bytes 131432216 | solution.py:241
  358.1 27.4 %gather_fusion.7 = bf16[4624,2,512]{2,1,0:T(2,128)(2,1)} fusion(bf16[2,135,512]{2,0,1:T(2,128)(2,1)S(1)} %concatenate.53.clone, s32[5120]{0:T(1024)S(1)} %pad_clamp_fusion.3), kind=kCustom, calls=%fused_computation.3 | custom fusion | bytes 18958400 | tf_op jit(solution)/shard_map/cond/branch_1_fun/gather | solution.py:39
  385.5 33.7 %fusion.165 = f32[2,68,512]{2,1,0:T(8,128)S(1)} fusion(bf16[92,512,512]{2,1,0:T(8,128)(2,1)} %get-tuple-element.269, bf16[2,68,68,512]{3,0,2,1:T(2,128)(2,1)} %bitcast.971, f32[512]{0:T(512)S(1)} %bitcast.1115), kind=kOutput, calls=%fused_computation.117 | convolution fusion | flops 4848685056 | bytes 45402112 | tf_op jit(solution)/shard_map/cond/branch_1_fun/btsd,sdo->bto/dot_general | solution.py:70
  450.9 87.1 %conditional.8 = (bf16[2,816,512]{2,1,0:T(8,128)(2,1)}, f32[2,816,512]{2,1,0:T(8,128)}, f32[2,68,512]{2,1,0:T(8,128)S(1)}, f32[2,68,512]{2,1,0:T(8,128)}) conditional(s32[]{:T(128)} %convert_element_type.450, (bf16[2,816,512]{2,0,1:T(2,128)(2,1)}, bf16[92,512,512]{2,1,0:T(8,128)(2,1)}, f32[4,512]{1,0:T(4,128)S(1)}, ...), branch_computations={%region_0.3_spmd, %region_3.6_spmd} | conditional | flops 6570222080 | bytes 131432216 | solution.py:241
  456.3 27.4 %gather_fusion.5 = bf16[4624,2,512]{2,1,0:T(2,128)(2,1)} fusion(bf16[2,135,512]{2,0,1:T(2,128)(2,1)S(1)} %concatenate.51.clone, s32[5120]{0:T(1024)S(1)} %pad_clamp_fusion.1), kind=kCustom, calls=%fused_computation.1 | custom fusion | bytes 18958400 | tf_op jit(solution)/shard_map/cond/branch_1_fun/gather | solution.py:39
  483.7 33.7 %fusion.79 = f32[2,68,512]{2,1,0:T(8,128)S(1)} fusion(bf16[92,512,512]{2,1,0:T(8,128)(2,1)} %get-tuple-element.261, bf16[2,68,68,512]{3,0,2,1:T(2,128)(2,1)} %bitcast.972, f32[512]{0:T(512)S(1)} %bitcast.1116), kind=kOutput, calls=%fused_computation.63 | convolution fusion | flops 4848685056 | bytes 45402112 | tf_op jit(solution)/shard_map/cond/branch_1_fun/btsd,sdo->bto/dot_general | solution.py:70
  580.5 61.1 %multiply_convert_fusion.2 = (bf16[816,2048]{1,0:T(8,128)(2,1)S(1)}, f32[816,2048]{1,0:T(8,128)}, bf16[816,2048]{1,0:T(8,128)(2,1)S(1)}, f32[816,2048]{1,0:T(8,1...) fusion(f32[2048]{0:T(1024)S(1)} %copy-done.153, f32[816,2048]{1,0:T(8,128)S(1)} %fusion.625, ...), kind=kOutput, calls=%fused_computation.503 | convolution fusion | flops 2044256256 | bytes 53922176 | tf_op jit(solution)/shard_map/btd,df->btf/dot_general | solution.py:254
  722.5 23.8 %all_to_all.99 = bf16[2,2,208896]{2,1,0:T(2,128)(2,1)S(1)} all-to-all(bf16[2,2,208896]{2,1,0:T(2,128)(2,1)} %reshape.2176), channel_id=1, replica_groups=mesh['branch'=2,'dp'=16] {'branch'}, dimensions={0} | all-to-all | bytes 3342336 | tf_op jit(solution)/shard_map/all_to_all | solution.py:295
  758.8 78.8 %conditional.13 = (f32[5,512]{1,0:T(8,128)S(1)}, bf16[2,68,512]{2,1,0:T(8,128)(2,1)S(1)}, bf16[2,68,512]{2,1,0:T(8,128)(2,1)S(1)}, bf16[2,816,512]{2,1,0:T(8,128...) conditional(s32[]{:T(128)} %convert_element_type.450, (f32[2,816,512]{2,1,0:T(8,128)}, ...), branch_computations={%region_84.94_spmd, %region_94.104_spmd} | conditional | flops 6586659328 | bytes 125944344 | solution.py:296
  780.9 27.4 %gather_fusion.15 = bf16[4624,2,512]{2,1,0:T(2,128)(2,1)} fusion(bf16[2,135,512]{2,0,1:T(2,128)(2,1)S(1)} %concatenate.61.clone, s32[5120]{0:T(1024)S(1)} %pad_clamp_fusion.11), kind=kCustom, calls=%fused_computation.11 | custom fusion | bytes 18958400 | tf_op jit(solution)/shard_map/cond/branch_1_fun/gather | solution.py:48
  870.8 22.9 all_to_all.100
  906.2 86.7 %conditional.11 = (f32[5,512]{1,0:T(8,128)S(1)}, bf16[2,68,512]{2,1,0:T(8,128)(2,1)S(1)}, bf16[2,68,512]{2,1,0:T(8,128)(2,1)S(1)}, bf16[2,816,512]{2,1,0:T(8,128...) conditional(s32[]{:T(128)} %convert_element_type.450, (f32[2,816,512]{2,1,0:T(8,128)}, ...), branch_computations={%region_34.44_spmd, %region_44.54_spmd} | conditional | flops 6586659328 | bytes 125944344 | solution.py:296
  936.0 27.4 %gather_fusion.11 = bf16[4624,2,512]{2,1,0:T(2,128)(2,1)} fusion(bf16[2,135,512]{2,0,1:T(2,128)(2,1)S(1)} %concatenate.57.clone, s32[5120]{0:T(1024)S(1)} %pad_clamp_fusion.7), kind=kCustom, calls=%fused_computation.7 | custom fusion | bytes 18958400 | tf_op jit(solution)/shard_map/cond/branch_1_fun/gather | solution.py:48
  1026.1 22.0 all_to_all.101
  1060.6 87.0 %conditional.12 = (f32[5,512]{1,0:T(8,128)S(1)}, bf16[2,68,512]{2,1,0:T(8,128)(2,1)}, bf16[2,68,512]{2,1,0:T(8,128)(2,1)S(1)}, bf16[2,816,512]{2,1,0:T(8,128)(2,...) conditional(s32[]{:T(128)} %convert_element_type.450, (f32[2,816,512]{2,1,0:T(8,128)}, ...), branch_computations={%region_59.69_spmd, %region_69.79_spmd} | conditional | flops 6586659328 | bytes 124838360 | solution.py:296
  1090.1 27.4 %gather_fusion.13 = bf16[4624,2,512]{2,1,0:T(2,128)(2,1)} fusion(bf16[2,135,512]{2,0,1:T(2,128)(2,1)S(1)} %concatenate.59.clone, s32[5120]{0:T(1024)S(1)} %pad_clamp_fusion.9), kind=kCustom, calls=%fused_computation.9 | custom fusion | bytes 18958400 | tf_op jit(solution)/shard_map/cond/branch_1_fun/gather | solution.py:48
  1117.5 19.9 convert_reduce_fusion.15
  1162.0 87.3 %conditional.15 = (f32[46,512,512]{2,1,0:T(8,128)}) conditional(s32[]{:T(128)} %convert_element_type.450, (bf16[6,68,512]{2,0,1:T(8,128)(2,1)S(1)}, bf16[6,68,512]{2,1,0:T(8,128)(2,1)S(1)}, bf16[6,816,512]{2,1,0:T(8,128)(2,1)}, bf16[6,68,512]{2,1,0:T(8,128)(2,1)S(1)}) %tuple.367, (bf16[6,68,512]{2,0,1:T(8,128)(2,1)S(1)}, ...), branch_computations={%region_108.109_spmd, %region_109.110_spmd} | conditional | flops 9851908096 | bytes 204500416 | solution.py:181
  1195.3 20.5 fusion.573
  1215.8 33.5 %pad_maximum_fusion.2 = f32[46,512,512]{2,1,0:T(8,128)} fusion(f32[12,512,512]{2,1,0:T(8,128)} %fusion.578, f32[34,512,512]{2,1,0:T(8,128)} %fusion.573), kind=kLoop, calls=%fused_computation.453 | loop fusion | flops 12058624 | bytes 96468992 | tf_op jit(solution)/shard_map/cond/branch_1_fun/concatenate | solution.py:175
  1251.2 112.8 %conditional.14 = (f32[46,512,512]{2,1,0:T(8,128)}) conditional(s32[]{:T(128)} %convert_element_type.450, (bf16[6,816,512]{2,1,0:T(8,128)(2,1)}, bf16[6,68,512]{2,1,0:T(8,128)(2,1)S(1)}, bf16[6,68,512]{2,0,1:T(8,128)(2,1)S(1)}, bf16[6,68,512]{2,1,0:T(8,128)(2,1)S(1)}) %tuple.369, (bf16[6,816,512]{2,1,0:T(8,128)(2,1)}, ...), branch_computations={%region_105.106_spmd, %region_106.107_spmd} | conditional | flops 9851908096 | bytes 204500128 | solution.py:181
  1269.6 28.5 %fusion.560 = f32[12,512,512]{2,1,0:T(8,128)} fusion(bf16[6,68,12,512]{3,2,1,0:T(8,128)(2,1)} %reshape.1923, bf16[6,68,512]{2,1,0:T(8,128)(2,1)S(1)} %get-tuple-element.321), kind=kOutput, calls=%fused_computation.436 | convolution fusion | flops 2566914048 | bytes 18014208 | tf_op jit(solution)/shard_map/cond/branch_1_fun/btrd,bto->rdo/dot_general | solution.py:145
  1309.6 20.8 fusion.555
  1330.4 33.3 %pad_maximum_fusion.1 = f32[46,512,512]{2,1,0:T(8,128)} fusion(f32[34,512,512]{2,1,0:T(8,128)} %fusion.555, f32[12,512,512]{2,1,0:T(8,128)} %fusion.560), kind=kLoop, calls=%fused_computation.430 | loop fusion | flops 12058624 | bytes 96468992 | tf_op jit(solution)/shard_map/cond/branch_1_fun/concatenate | solution.py:175
  1397.2 45.0 %all-reduce.28 = (f32[2,5,512]{2,1,0:T(8,128)S(1)}, f32[2048]{0:T(1024)}, f32[4,512]{1,0:T(4,128)}, f32[2,512]{1,0:T(2,128)}) all-reduce(f32[2,5,512]{2,1,0:T(8,128)S(1)} %broadcast_select_fusion, f32[2048]{0:T(1024)S(1)} %add_add_fusion.19, f32[4,512]{1,0:T(4,128)S(1)} %fusion.613, ...), channel_id=1, replica_groups=mesh['branch'=2,'dp'=16] {'branch','dp'}, use_global_device_ids=true, to_apply=%region_111.112 | all-reduce | flops 10240 | bytes 81920 | tf_op jit(solution)/shard_map/psum | solution.py:336
  1446.8 253.1 %reduce-scatter.14.cloned.1.call-done = f32[1472,512]{1,0:T(8,128)} async-done(((f32[23552,512]{1,0:T(8,128)}), f32[1472,512]{1,0:T(8,128)}) %reduce-scatter.14.cloned.1.call-update) | async-done | bytes 3014672 | tf_op jit(solution)/shard_map/reduce_scatter | solution.py:334
  1699.9 453.7 %reduce-scatter.12.cloned.1.call-done = f32[1472,512]{1,0:T(8,128)} async-done(((f32[23552,512]{1,0:T(8,128)}), f32[1472,512]{1,0:T(8,128)}) %reduce-scatter.12.cloned.1.call-update) | async-done | bytes 3014672 | tf_op jit(solution)/shard_map/reduce_scatter | solution.py:334
  2159.7 203.9 %all-reduce.32.cloned.1.call-done = (f32[1024,512]{1,0:T(8,128)}, f32[512,2048]{1,0:T(8,128)}, f32[2048,512]{1,0:T(8,128)}) async-done(((f32[1024,512]{1,0:T(8,128)}, f32[512,2048]{1,0:T(8,128)}, f32[2048,512]{1,0:T(8,128)}), (f32[1024,512]{1,0:T(8,128)}, f32[512,2048]{1,0:T(8,128)}, f32[2048,512]{1,0:T(8,128)})) %all-reduce.32.cloned.1.call-update) | async-done | bytes 10485776 | tf_op jit(solution)/shard_map/psum | solution.py:336
  (586 shorter events, 585.0 us)
Async XLA Ops:
  7.2 568.0 %copy-start = (bf16[512,2048]{1,0:T(8,128)(2,1)S(1)}, bf16[512,2048]{1,0:T(8,128)(2,1)}, u32[]{:S(2)}) copy-start(bf16[512,2048]{1,0:T(8,128)(2,1)} %param.34) | copy-start | bytes 6291460
  7.2 242.3 %all-gather.2.cloned.1.call-start = ((), (), s32[]{:S(2)}) async-start(), calls=%async_computation.11 | async-start | bytes 51249152 | tf_op jit(solution)/shard_map/all_gather | solution.py:213
  12.7 236.8 %copy-start.71 = (f32[1,512]{1,0:T(1,128)S(1)}, f32[1,512]{1,0:T(1,128)}, u32[]{:S(2)}) copy-start(f32[1,512]{1,0:T(1,128)} %param.31) | copy-start | bytes 6148
  12.7 236.8 %copy-start.87 = (f32[1,4,512]{2,1,0:T(4,128)S(1)}, f32[1,4,512]{2,1,0:T(4,128)}, u32[]{:S(2)}) copy-start(f32[1,4,512]{2,1,0:T(4,128)} %param.32) | copy-start | bytes 24580
  343.8 96.1 %all-to-all-start.2 = ((bf16[2,816,512]{2,1,0:T(8,128)(2,1)}), bf16[2,816,512]{2,1,0:T(8,128)(2,1)}, u32[]{:S(2)}, u32[]{:S(2)}) async-start(bf16[2,816,512]{2,1,0:T(8,128)(2,1)} %get-tuple-element.375), calls=%async_computation.2 | async-start | bytes 3342336 | tf_op jit(solution)/shard_map/all_to_all | solution.py:244
  439.9 104.1 %all-to-all-start.1 = ((bf16[2,816,512]{2,1,0:T(8,128)(2,1)}), bf16[2,816,512]{2,1,0:T(8,128)(2,1)}, u32[]{:S(2)}, u32[]{:S(2)}) async-start(bf16[2,816,512]{2,1,0:T(8,128)(2,1)} %get-tuple-element.374), calls=%async_computation.1 | async-start | bytes 3342336 | tf_op jit(solution)/shard_map/all_to_all | solution.py:244
  445.3 247.5 %copy-start.88 = (f32[1,512]{1,0:T(1,128)}, f32[1,512]{1,0:T(1,128)S(1)}, u32[]{:S(2)}) copy-start(f32[1,512]{1,0:T(1,128)S(1)} %get-tuple-element.817) | copy-start | bytes 6148
  450.9 128.7 %copy-start.95 = (f32[1,512]{1,0:T(1,128)}, f32[1,512]{1,0:T(1,128)S(1)}, u32[]{:S(2)}) copy-start(f32[1,512]{1,0:T(1,128)S(1)} %get-tuple-element.813) | copy-start | bytes 6148
  544.1 33.5 %copy-start.110 = (f32[816]{0:T(1024)}, f32[816]{0:T(1024)S(1)}, u32[]{:S(2)}) copy-start(f32[816]{0:T(1024)S(1)} %broadcast_multiply_fusion.13) | copy-start | bytes 9796
  544.1 25.7 %all-to-all-start = ((bf16[2,816,512]{2,1,0:T(8,128)(2,1)}), bf16[2,816,512]{2,1,0:T(8,128)(2,1)}, u32[]{:S(2)}, u32[]{:S(2)}) async-start(bf16[2,816,512]{2,1,0:T(8,128)(2,1)} %get-tuple-element.373), calls=%async_computation | async-start | bytes 3342336 | tf_op jit(solution)/shard_map/all_to_all | solution.py:244
  548.8 894.6 %reduce-scatter.10.cloned.1.call-start = ((), (), s32[]{:S(2)}) async-start(), calls=%async_computation.14 | async-start | bytes 2506752 | tf_op jit(solution)/shard_map/reduce_scatter | solution.py:310
  554.1 21.1 copy-start.90
  555.3 18.2 copy-start.113
  555.7 17.9 copy-start.115
  555.7 21.9 copy-start.123
  555.7 19.5 copy-start.97
  574.7 118.1 %copy-start.13 = (f32[816,512]{1,0:T(8,128)}, f32[816,512]{1,0:T(8,128)S(1)}, u32[]{:S(2)}) copy-start(f32[816,512]{1,0:T(8,128)S(1)} %get-tuple-element.829) | copy-start | bytes 5013508
  574.7 118.1 %copy-start.93 = (f32[816]{0:T(1024)}, f32[816]{0:T(1024)S(1)}, u32[]{:S(2)}) copy-start(f32[816]{0:T(1024)S(1)} %broadcast_multiply_fusion.17) | copy-start | bytes 9796
  575.1 117.7 %copy-start.100 = (f32[816]{0:T(1024)}, f32[816]{0:T(1024)S(1)}, u32[]{:S(2)}) copy-start(f32[816]{0:T(1024)S(1)} %fusion.615) | copy-start | bytes 9796
  580.5 61.1 %copy-start.154 = (f32[816,2048]{1,0:T(8,128)}, f32[816,2048]{1,0:T(8,128)S(1)}, u32[]{:S(2)}) copy-start(f32[816,2048]{1,0:T(8,128)S(1)} %fusion.625) | copy-start | bytes 20054020
  580.5 61.2 %copy-start.147 = (f32[1,512]{1,0:T(1,128)S(1)}, f32[1,512]{1,0:T(1,128)}, u32[]{:S(2)}) copy-start(f32[1,512]{1,0:T(1,128)} %get-tuple-element.815) | copy-start | bytes 6148
  580.5 61.2 %copy-start.148 = (bf16[2048,512]{1,0:T(8,128)(2,1)S(1)}, bf16[2048,512]{1,0:T(8,128)(2,1)}, u32[]{:S(2)}) copy-start(bf16[2048,512]{1,0:T(8,128)(2,1)} %param.36) | copy-start | bytes 6291460
  656.4 23.4 copy-start.21
  656.4 10.5 copy-start.119
  780.6 27.7 %copy-start.55 = (bf16[2,68,512]{2,1,0:T(8,128)(2,1)}, bf16[2,68,512]{2,1,0:T(8,128)(2,1)S(1)}, u32[]{:S(2)}) copy-start(bf16[2,68,512]{2,1,0:T(8,128)(2,1)S(1)} %get-tuple-element.882) | copy-start | bytes 417796 | tf_op jit(solution)/shard_map/cond
  842.6 600.8 %reduce-scatter.6.cloned.1.call-start = ((), (), s32[]{:S(2)}) async-start(), calls=%async_computation.12 | async-start | bytes 2506752 | tf_op jit(solution)/shard_map/reduce_scatter | solution.py:310
  935.6 27.7 %copy-start.59 = (bf16[2,68,512]{2,1,0:T(8,128)(2,1)}, bf16[2,68,512]{2,1,0:T(8,128)(2,1)S(1)}, u32[]{:S(2)}) copy-start(bf16[2,68,512]{2,1,0:T(8,128)(2,1)S(1)} %get-tuple-element.906) | copy-start | bytes 417796 | tf_op jit(solution)/shard_map/cond
  997.9 445.5 %reduce-scatter.8.cloned.1.call-start = ((), (), s32[]{:S(2)}) async-start(), calls=%async_computation.13 | async-start | bytes 2506752 | tf_op jit(solution)/shard_map/reduce_scatter | solution.py:310
  1089.8 27.7 %copy-start.61 = (bf16[2,68,512]{2,1,0:T(8,128)(2,1)}, bf16[2,68,512]{2,1,0:T(8,128)(2,1)S(1)}, u32[]{:S(2)}) copy-start(bf16[2,68,512]{2,1,0:T(8,128)(2,1)S(1)} %get-tuple-element.894) | copy-start | bytes 417796 | tf_op jit(solution)/shard_map/cond
  1152.4 547.5 %reduce-scatter.14.cloned.1.call-start = ((), (), s32[]{:S(2)}) async-start(), calls=%async_computation.16 | async-start | bytes 51249152 | tf_op jit(solution)/shard_map/reduce_scatter | solution.py:334
  1249.3 904.3 %reduce-scatter.12.cloned.1.call-start = ((), (), s32[]{:S(2)}) async-start(), calls=%async_computation.15 | async-start | bytes 51249152 | tf_op jit(solution)/shard_map/reduce_scatter | solution.py:334
  1364.1 999.4 %all-reduce.32.cloned.1.call-start = ((), (), s32[]{:S(2)}) async-start(), calls=%async_computation.17 | async-start | bytes 20971520 | tf_op jit(solution)/shard_map/psum | solution.py:336
  (134 other events, 505.4 us)
Sparse Core Ops, SparseCore 0:
  9.6 239.8 all-gather.1
  842.7 26.2 reduce-scatter.9
  998.0 26.2 reduce-scatter.5
  1152.5 26.2 reduce-scatter.7
  1249.4 450.4 reduce-scatter.13
  1704.7 448.9 reduce-scatter.11
  2160.9 202.6 all-reduce.31
where the time goes:
time: 2390 us; the launch traced here: 2380 us
  waiting for transfers between devices  1160 us (49%)
  matrix products  437 us (18%)
  local copies, waits for them, and re-layouts  374 us (16%)
  other arithmetic  227 us (9%)
  blocking collectives  114 us (5%)
  loops' own time  35.9 us (2%)
    reduce_scatter x2, waiting for transfers between devices, per_device(): lax.psum_scatter(term, 'dp', scatter_dimension=0, tiled=True)  707 us
    all_gather x1, waiting for transfers between devices, per_device(): gathered = lax.all_gather(branch_blocks, 'dp', axis=2, tiled=True)  234 us
    psum x1, waiting for transfers between devices, per_device(): lax.psum((shared_totals[0], shared_totals[1], shared_totals[2], shared_to...  204 us
    gather x5, local copies, waits for them, and re-layouts, past_windows(): return padded[:, offsets, :]  104 us
    dot_general x3, matrix products, branch_forward(): jnp.einsum('btsd,sdo->bto', windows, iso_weight, preferred_element_type=j...  101 us
    gather x3, local copies, waits for them, and re-layouts, future_windows(): return padded[:, offsets, :]  82.2 us
    unnamed x301, local copies, waits for them, and re-layouts  69.1 us
    all_to_all x3, blocking collectives, per_device(): lax.all_to_all(grad_joined, 'branch', split_axis=2, concat_axis=0, tiled=...  68.8 us
  transfers between devices with their start and end apart: 10, of which 5 were waited for; matrix products, arithmetic and copies ran while one was open for 29% of the time, Pallas kernels for 0%

commit v1 on v0

--- a/solution.py
+++ b/solution.py
@@ -292,7 +292,10 @@
             jnp.stack([grad_gain_one, grad_gain_two]),
         )
         shared_totals = [running + addend for running, addend in zip(shared_totals, terms)]
-        grad_branch = lax.all_to_all(grad_joined, "branch", split_axis=2, concat_axis=0, tiled=True)
+        size = lax.axis_size("branch")
+        parts = jnp.stack(jnp.split(grad_joined, size, axis=2), axis=0)
+        parts = lax.all_to_all(parts, "branch", split_axis=0, concat_axis=0)
+        grad_branch = jnp.concatenate(parts, axis=0)
         grad_values, vectors, grad_down, grad_iso, grad_expanded = lax.cond(
             branch_index == 0,
             backward_pair[0],

time: 2390 us -> 2310 us (0.967)
  local copies, waits for them, and re-layouts: 374 us -> 301 us
  other arithmetic: 227 us -> 194 us
  blocking collectives: 114 us -> 143 us
    unnamed x301 -> x291, local copies, waits for them, and re-layouts: 69.1 us -> 29.5 us
    unnamed x4 -> x1, other arithmetic: 37 us -> 1.73 us
    all_to_all x3, blocking collectives: 68.8 us -> 98.9 us  [per_device(): parts = lax.all_to_all(parts, 'branch', split_axis=0, concat_axis=0)]
  transfers between devices with their start and end apart: 10 -> 10, of which waited for: 5 -> 5; matrix products, arithmetic and copies ran while one was open for 29% -> 27% of each run, Pallas kernels for 0% -> 0%
where the time goes in v1:
time: 2310 us; the launch traced here: 2300 us
  waiting for transfers between devices  1160 us (50%)
  matrix products  437 us (19%)
  local copies, waits for them, and re-layouts  301 us (13%)
  other arithmetic  194 us (8%)
  blocking collectives  143 us (6%)
  loops' own time  35.8 us (2%)
    reduce_scatter x2, waiting for transfers between devices, per_device(): lax.psum_scatter(term, 'dp', scatter_dimension=0, tiled=True)  710 us
    all_gather x1, waiting for transfers between devices, per_device(): gathered = lax.all_gather(branch_blocks, 'dp', axis=2, tiled=True)  234 us
    psum x1, waiting for transfers between devices, per_device(): lax.psum((shared_totals[0], shared_totals[1], shared_totals[2], shared_to...  204 us
    gather x5, local copies, waits for them, and re-layouts, past_windows(): return padded[:, offsets, :]  104 us
    dot_general x3, matrix products, branch_forward(): jnp.einsum('btsd,sdo->bto', windows, iso_weight, preferred_element_type=j...  101 us
    all_to_all x3, blocking collectives, per_device(): parts = lax.all_to_all(parts, 'branch', split_axis=0, concat_axis=0)  98.9 us
    gather x3, local copies, waits for them, and re-layouts, future_windows(): return padded[:, offsets, :]  82.2 us
    concatenate x2, other arithmetic, group_grads(): jnp.concatenate(pieces, axis=0).reshape(per_group * channels, channels)  67 us
  transfers between devices with their start and end apart: 10, of which 5 were waited for; matrix products, arithmetic and copies ran while one was open for 27% of the time, Pallas kernels for 0%

profile of v1, /device:TPU:0, one launch (start us, length us, event | category | flops | bytes accessed | tf_op | source)
XLA Modules:
  0.0 2304.9 jit_solution(14280436743063928825)
XLA Ops:
  15.6 233.9 %all-gather.2.cloned.1.call-done = bf16[1,2,23552,512]{3,2,1,0:T(8,128)(2,1)} async-done(((bf16[1,2,1472,512]{3,2,1,0:T(8,128)(2,1)}), bf16[1,2,23552,512]{3,2,1,0:T(8,128)(2,1)}) %all-gather.2.cloned.1.call-update) | async-done | bytes 48234512 | tf_op jit(solution)/shard_map/all_gather | solution.py:213
  249.5 94.2 %conditional.10 = (bf16[2,816,512]{2,1,0:T(8,128)(2,1)}, f32[2,816,512]{2,1,0:T(8,128)}, f32[2,68,512]{2,1,0:T(8,128)S(1)}, f32[2,68,512]{2,1,0:T(8,128)}) conditional(s32[]{:T(128)} %convert_element_type.450, (bf16[2,816,512]{2,0,1:T(2,128)(2,1)}, bf16[92,512,512]{2,1,0:T(8,128)(2,1)}, f32[4,512]{1,0:T(4,128)S(1)}, ...), branch_computations={%region_20.0_spmd, %region_23.0_spmd} | conditional | flops 6570222080 | bytes 131432216 | solution.py:241
  262.0 27.4 %gather_fusion.9 = bf16[4624,2,512]{2,1,0:T(2,128)(2,1)} fusion(bf16[2,135,512]{2,0,1:T(2,128)(2,1)S(1)} %concatenate.55.clone, s32[5120]{0:T(1024)S(1)} %pad_clamp_fusion.5), kind=kCustom, calls=%fused_computation.5 | custom fusion | bytes 18958400 | tf_op jit(solution)/shard_map/cond/branch_1_fun/gather | solution.py:39
  289.4 33.7 %fusion.251 = f32[2,68,512]{2,1,0:T(8,128)S(1)} fusion(bf16[92,512,512]{2,1,0:T(8,128)(2,1)} %get-tuple-element.277, bf16[2,68,68,512]{3,0,2,1:T(2,128)(2,1)} %bitcast.961, f32[512]{0:T(512)S(1)} %bitcast.1102), kind=kOutput, calls=%fused_computation.171 | convolution fusion | flops 4848685056 | bytes 45402112 | tf_op jit(solution)/shard_map/cond/branch_1_fun/btsd,sdo->bto/dot_general | solution.py:70
  352.8 87.1 %conditional.9 = (bf16[2,816,512]{2,1,0:T(8,128)(2,1)}, f32[2,816,512]{2,1,0:T(8,128)}, f32[2,68,512]{2,1,0:T(8,128)S(1)}, f32[2,68,512]{2,1,0:T(8,128)}) conditional(s32[]{:T(128)} %convert_element_type.450, (bf16[2,816,512]{2,0,1:T(2,128)(2,1)}, bf16[92,512,512]{2,1,0:T(8,128)(2,1)}, f32[4,512]{1,0:T(4,128)S(1)}, ...), branch_computations={%region_10.0_spmd, %region_13.0_spmd} | conditional | flops 6570222080 | bytes 131432216 | solution.py:241
  358.1 27.4 %gather_fusion.7 = bf16[4624,2,512]{2,1,0:T(2,128)(2,1)} fusion(bf16[2,135,512]{2,0,1:T(2,128)(2,1)S(1)} %concatenate.53.clone, s32[5120]{0:T(1024)S(1)} %pad_clamp_fusion.3), kind=kCustom, calls=%fused_computation.3 | custom fusion | bytes 18958400 | tf_op jit(solution)/shard_map/cond/branch_1_fun/gather | solution.py:39
  385.5 33.7 %fusion.165 = f32[2,68,512]{2,1,0:T(8,128)S(1)} fusion(bf16[92,512,512]{2,1,0:T(8,128)(2,1)} %get-tuple-element.269, bf16[2,68,68,512]{3,0,2,1:T(2,128)(2,1)} %bitcast.962, f32[512]{0:T(512)S(1)} %bitcast.1103), kind=kOutput, calls=%fused_computation.117 | convolution fusion | flops 4848685056 | bytes 45402112 | tf_op jit(solution)/shard_map/cond/branch_1_fun/btsd,sdo->bto/dot_general | solution.py:70
  450.9 87.1 %conditional.8 = (bf16[2,816,512]{2,1,0:T(8,128)(2,1)}, f32[2,816,512]{2,1,0:T(8,128)}, f32[2,68,512]{2,1,0:T(8,128)S(1)}, f32[2,68,512]{2,1,0:T(8,128)}) conditional(s32[]{:T(128)} %convert_element_type.450, (bf16[2,816,512]{2,0,1:T(2,128)(2,1)}, bf16[92,512,512]{2,1,0:T(8,128)(2,1)}, f32[4,512]{1,0:T(4,128)S(1)}, ...), branch_computations={%region_0.3_spmd, %region_3.6_spmd} | conditional | flops 6570222080 | bytes 131432216 | solution.py:241
  456.3 27.4 %gather_fusion.5 = bf16[4624,2,512]{2,1,0:T(2,128)(2,1)} fusion(bf16[2,135,512]{2,0,1:T(2,128)(2,1)S(1)} %concatenate.51.clone, s32[5120]{0:T(1024)S(1)} %pad_clamp_fusion.1), kind=kCustom, calls=%fused_computation.1 | custom fusion | bytes 18958400 | tf_op jit(solution)/shard_map/cond/branch_1_fun/gather | solution.py:39
  483.7 33.7 %fusion.79 = f32[2,68,512]{2,1,0:T(8,128)S(1)} fusion(bf16[92,512,512]{2,1,0:T(8,128)(2,1)} %get-tuple-element.261, bf16[2,68,68,512]{3,0,2,1:T(2,128)(2,1)} %bitcast.963, f32[512]{0:T(512)S(1)} %bitcast.1104), kind=kOutput, calls=%fused_computation.63 | convolution fusion | flops 4848685056 | bytes 45402112 | tf_op jit(solution)/shard_map/cond/branch_1_fun/btsd,sdo->bto/dot_general | solution.py:70
  580.5 61.1 %multiply_convert_fusion.2 = (bf16[816,2048]{1,0:T(8,128)(2,1)S(1)}, f32[816,2048]{1,0:T(8,128)}, bf16[816,2048]{1,0:T(8,128)(2,1)S(1)}, f32[816,2048]{1,0:T(8,1...) fusion(f32[2048]{0:T(1024)S(1)} %copy-done.153, f32[816,2048]{1,0:T(8,128)S(1)} %fusion.625, ...), kind=kOutput, calls=%fused_computation.503 | convolution fusion | flops 2044256256 | bytes 53922176 | tf_op jit(solution)/shard_map/btd,df->btf/dot_general | solution.py:254
  698.4 22.6 all_to_all.60
  721.1 79.3 %conditional.12 = (f32[5,512]{1,0:T(8,128)S(1)}, bf16[2,68,512]{2,1,0:T(8,128)(2,1)S(1)}, bf16[2,68,512]{2,1,0:T(8,128)(2,1)S(1)}, bf16[2,816,512]{2,1,0:T(8,128...) conditional(s32[]{:T(128)} %convert_element_type.450, (f32[2,816,512]{2,1,0:T(8,128)}, ...), branch_computations={%region_59.69_spmd, %region_69.79_spmd} | conditional | flops 6586659328 | bytes 125944344 | solution.py:299
  743.4 27.4 %gather_fusion.13 = bf16[4624,2,512]{2,1,0:T(2,128)(2,1)} fusion(bf16[2,135,512]{2,0,1:T(2,128)(2,1)S(1)} %concatenate.59.clone, s32[5120]{0:T(1024)S(1)} %pad_clamp_fusion.9), kind=kCustom, calls=%fused_computation.9 | custom fusion | bytes 18958400 | tf_op jit(solution)/shard_map/cond/branch_1_fun/gather | solution.py:48
  810.6 37.7 %all_to_all.61 = bf16[2,1,816,512]{3,2,1,0:T(8,128)(2,1)S(1)} all-to-all(bf16[2,1,816,512]{3,2,1,0:T(8,128)(2,1)S(1)} %pad_maximum_fusion.4), channel_id=1, replica_groups=mesh['branch'=2,'dp'=16] {'branch'}, dimensions={0} | all-to-all | bytes 3342336 | tf_op jit(solution)/shard_map/all_to_all | solution.py:297
  848.3 87.2 %conditional.11 = (f32[5,512]{1,0:T(8,128)S(1)}, bf16[2,68,512]{2,1,0:T(8,128)(2,1)S(1)}, bf16[2,68,512]{2,1,0:T(8,128)(2,1)S(1)}, bf16[2,816,512]{2,1,0:T(8,128...) conditional(s32[]{:T(128)} %convert_element_type.450, (f32[2,816,512]{2,1,0:T(8,128)}, ...), branch_computations={%region_34.44_spmd, %region_44.54_spmd} | conditional | flops 6586659328 | bytes 125944344 | solution.py:299
  878.5 27.4 %gather_fusion.11 = bf16[4624,2,512]{2,1,0:T(2,128)(2,1)} fusion(bf16[2,135,512]{2,0,1:T(2,128)(2,1)S(1)} %concatenate.57.clone, s32[5120]{0:T(1024)S(1)} %pad_clamp_fusion.7), kind=kCustom, calls=%fused_computation.7 | custom fusion | bytes 18958400 | tf_op jit(solution)/shard_map/cond/branch_1_fun/gather | solution.py:48
  945.8 38.5 %all_to_all.62 = bf16[2,1,816,512]{3,2,1,0:T(8,128)(2,1)S(1)} all-to-all(bf16[2,1,816,512]{3,2,1,0:T(8,128)(2,1)S(1)} %pad_maximum_fusion.6), channel_id=1, replica_groups=mesh['branch'=2,'dp'=16] {'branch'}, dimensions={0} | all-to-all | bytes 3342336 | tf_op jit(solution)/shard_map/all_to_all | solution.py:297
  984.4 87.8 %conditional.13 = (f32[5,512]{1,0:T(8,128)S(1)}, bf16[2,68,512]{2,1,0:T(8,128)(2,1)}, bf16[2,68,512]{2,1,0:T(8,128)(2,1)S(1)}, bf16[2,816,512]{2,1,0:T(8,128)(2,...) conditional(s32[]{:T(128)} %convert_element_type.450, (f32[2,816,512]{2,1,0:T(8,128)}, ...), branch_computations={%region_84.94_spmd, %region_94.104_spmd} | conditional | flops 6586659328 | bytes 124838360 | solution.py:299
  1014.6 27.4 %gather_fusion.15 = bf16[4624,2,512]{2,1,0:T(2,128)(2,1)} fusion(bf16[2,135,512]{2,0,1:T(2,128)(2,1)S(1)} %concatenate.61.clone, s32[5120]{0:T(1024)S(1)} %pad_clamp_fusion.11), kind=kCustom, calls=%fused_computation.11 | custom fusion | bytes 18958400 | tf_op jit(solution)/shard_map/cond/branch_1_fun/gather | solution.py:48
  1042.0 20.0 convert_reduce_fusion.23
  1086.2 87.3 %conditional.15 = (f32[46,512,512]{2,1,0:T(8,128)}) conditional(s32[]{:T(128)} %convert_element_type.450, (bf16[6,68,512]{2,0,1:T(8,128)(2,1)S(1)}, bf16[6,68,512]{2,1,0:T(8,128)(2,1)S(1)}, bf16[6,816,512]{2,1,0:T(8,128)(2,1)}, bf16[6,68,512]{2,1,0:T(8,128)(2,1)S(1)}) %tuple.344, (bf16[6,68,512]{2,0,1:T(8,128)(2,1)S(1)}, ...), branch_computations={%region_108.109_spmd, %region_109.110_spmd} | conditional | flops 9851908096 | bytes 204500416 | solution.py:181
  1119.5 20.5 fusion.573
  1140.0 33.5 %pad_maximum_fusion.2 = f32[46,512,512]{2,1,0:T(8,128)} fusion(f32[12,512,512]{2,1,0:T(8,128)} %fusion.578, f32[34,512,512]{2,1,0:T(8,128)} %fusion.573), kind=kLoop, calls=%fused_computation.453 | loop fusion | flops 12058624 | bytes 96468992 | tf_op jit(solution)/shard_map/cond/branch_1_fun/concatenate | solution.py:175
  1175.5 113.0 %conditional.14 = (f32[46,512,512]{2,1,0:T(8,128)}) conditional(s32[]{:T(128)} %convert_element_type.450, (bf16[6,816,512]{2,1,0:T(8,128)(2,1)}, bf16[6,68,512]{2,1,0:T(8,128)(2,1)S(1)}, bf16[6,68,512]{2,0,1:T(8,128)(2,1)S(1)}, bf16[6,68,512]{2,1,0:T(8,128)(2,1)S(1)}) %tuple.346, (bf16[6,816,512]{2,1,0:T(8,128)(2,1)}, ...), branch_computations={%region_105.106_spmd, %region_106.107_spmd} | conditional | flops 9851908096 | bytes 204500128 | solution.py:181
  1193.8 28.2 %fusion.560 = f32[12,512,512]{2,1,0:T(8,128)} fusion(bf16[6,68,12,512]{3,2,1,0:T(8,128)(2,1)} %reshape.1929, bf16[6,68,512]{2,1,0:T(8,128)(2,1)S(1)} %get-tuple-element.321), kind=kOutput, calls=%fused_computation.436 | convolution fusion | flops 2566914048 | bytes 18014208 | tf_op jit(solution)/shard_map/cond/branch_1_fun/btrd,bto->rdo/dot_general | solution.py:145
  1233.7 20.8 fusion.555
  1254.5 33.5 %pad_maximum_fusion.1 = f32[46,512,512]{2,1,0:T(8,128)} fusion(f32[34,512,512]{2,1,0:T(8,128)} %fusion.555, f32[12,512,512]{2,1,0:T(8,128)} %fusion.560), kind=kLoop, calls=%fused_computation.430 | loop fusion | flops 12058624 | bytes 96468992 | tf_op jit(solution)/shard_map/cond/branch_1_fun/concatenate | solution.py:175
  1320.6 43.9 %all-reduce.28 = (f32[2,5,512]{2,1,0:T(8,128)S(1)}, f32[2048]{0:T(1024)}, f32[4,512]{1,0:T(4,128)}, f32[2,512]{1,0:T(2,128)}) all-reduce(f32[2,5,512]{2,1,0:T(8,128)S(1)} %broadcast_select_fusion, f32[2048]{0:T(1024)S(1)} %add_add_fusion.19, f32[4,512]{1,0:T(4,128)S(1)} %fusion.613, ...), channel_id=1, replica_groups=mesh['branch'=2,'dp'=16] {'branch','dp'}, use_global_device_ids=true, to_apply=%region_111.112 | all-reduce | flops 10240 | bytes 81920 | tf_op jit(solution)/shard_map/psum | solution.py:339
  1369.2 255.5 %reduce-scatter.14.cloned.1.call-done = f32[1472,512]{1,0:T(8,128)} async-done(((f32[23552,512]{1,0:T(8,128)}), f32[1472,512]{1,0:T(8,128)}) %reduce-scatter.14.cloned.1.call-update) | async-done | bytes 3014672 | tf_op jit(solution)/shard_map/reduce_scatter | solution.py:337
  1624.7 454.2 %reduce-scatter.12.cloned.1.call-done = f32[1472,512]{1,0:T(8,128)} async-done(((f32[23552,512]{1,0:T(8,128)}), f32[1472,512]{1,0:T(8,128)}) %reduce-scatter.12.cloned.1.call-update) | async-done | bytes 3014672 | tf_op jit(solution)/shard_map/reduce_scatter | solution.py:337
  2085.0 203.9 %all-reduce.32.cloned.1.call-done = (f32[1024,512]{1,0:T(8,128)}, f32[512,2048]{1,0:T(8,128)}, f32[2048,512]{1,0:T(8,128)}) async-done(((f32[1024,512]{1,0:T(8,128)}, f32[512,2048]{1,0:T(8,128)}, f32[2048,512]{1,0:T(8,128)}), (f32[1024,512]{1,0:T(8,128)}, f32[512,2048]{1,0:T(8,128)}, f32[2048,512]{1,0:T(8,128)})) %all-reduce.32.cloned.1.call-update) | async-done | bytes 10485776 | tf_op jit(solution)/shard_map/psum | solution.py:339
  (573 shorter events, 478.5 us)
Async XLA Ops:
  7.2 568.0 %copy-start = (bf16[512,2048]{1,0:T(8,128)(2,1)S(1)}, bf16[512,2048]{1,0:T(8,128)(2,1)}, u32[]{:S(2)}) copy-start(bf16[512,2048]{1,0:T(8,128)(2,1)} %param.34) | copy-start | bytes 6291460
  7.2 242.3 %all-gather.2.cloned.1.call-start = ((), (), s32[]{:S(2)}) async-start(), calls=%async_computation.11 | async-start | bytes 51249152 | tf_op jit(solution)/shard_map/all_gather | solution.py:213
  12.7 236.8 %copy-start.71 = (f32[1,512]{1,0:T(1,128)S(1)}, f32[1,512]{1,0:T(1,128)}, u32[]{:S(2)}) copy-start(f32[1,512]{1,0:T(1,128)} %param.31) | copy-start | bytes 6148
  12.7 236.8 %copy-start.87 = (f32[1,4,512]{2,1,0:T(4,128)S(1)}, f32[1,4,512]{2,1,0:T(4,128)}, u32[]{:S(2)}) copy-start(f32[1,4,512]{2,1,0:T(4,128)} %param.32) | copy-start | bytes 24580
  343.8 96.1 %all-to-all-start.2 = ((bf16[2,816,512]{2,1,0:T(8,128)(2,1)}), bf16[2,816,512]{2,1,0:T(8,128)(2,1)}, u32[]{:S(2)}, u32[]{:S(2)}) async-start(bf16[2,816,512]{2,1,0:T(8,128)(2,1)} %get-tuple-element.375), calls=%async_computation.2 | async-start | bytes 3342336 | tf_op jit(solution)/shard_map/all_to_all | solution.py:244
  439.9 104.1 %all-to-all-start.1 = ((bf16[2,816,512]{2,1,0:T(8,128)(2,1)}), bf16[2,816,512]{2,1,0:T(8,128)(2,1)}, u32[]{:S(2)}, u32[]{:S(2)}) async-start(bf16[2,816,512]{2,1,0:T(8,128)(2,1)} %get-tuple-element.374), calls=%async_computation.1 | async-start | bytes 3342336 | tf_op jit(solution)/shard_map/all_to_all | solution.py:244
  445.3 246.6 %copy-start.88 = (f32[1,512]{1,0:T(1,128)}, f32[1,512]{1,0:T(1,128)S(1)}, u32[]{:S(2)}) copy-start(f32[1,512]{1,0:T(1,128)S(1)} %get-tuple-element.681) | copy-start | bytes 6148
  450.9 128.7 %copy-start.95 = (f32[1,512]{1,0:T(1,128)}, f32[1,512]{1,0:T(1,128)S(1)}, u32[]{:S(2)}) copy-start(f32[1,512]{1,0:T(1,128)S(1)} %get-tuple-element.677) | copy-start | bytes 6148
  544.1 33.5 %copy-start.110 = (f32[816]{0:T(1024)}, f32[816]{0:T(1024)S(1)}, u32[]{:S(2)}) copy-start(f32[816]{0:T(1024)S(1)} %broadcast_multiply_fusion.13) | copy-start | bytes 9796
  544.1 25.7 %all-to-all-start = ((bf16[2,816,512]{2,1,0:T(8,128)(2,1)}), bf16[2,816,512]{2,1,0:T(8,128)(2,1)}, u32[]{:S(2)}, u32[]{:S(2)}) async-start(bf16[2,816,512]{2,1,0:T(8,128)(2,1)} %get-tuple-element.373), calls=%async_computation | async-start | bytes 3342336 | tf_op jit(solution)/shard_map/all_to_all | solution.py:244
  548.7 816.9 %reduce-scatter.8.cloned.1.call-start = ((), (), s32[]{:S(2)}) async-start(), calls=%async_computation.13 | async-start | bytes 2506752 | tf_op jit(solution)/shard_map/reduce_scatter | solution.py:313
  574.7 117.2 %copy-start.13 = (f32[816,512]{1,0:T(8,128)}, f32[816,512]{1,0:T(8,128)S(1)}, u32[]{:S(2)}) copy-start(f32[816,512]{1,0:T(8,128)S(1)} %get-tuple-element.693) | copy-start | bytes 5013508
  574.7 117.2 %copy-start.93 = (f32[816]{0:T(1024)}, f32[816]{0:T(1024)S(1)}, u32[]{:S(2)}) copy-start(f32[816]{0:T(1024)S(1)} %broadcast_multiply_fusion.17) | copy-start | bytes 9796
  575.1 116.8 %copy-start.100 = (f32[816]{0:T(1024)}, f32[816]{0:T(1024)S(1)}, u32[]{:S(2)}) copy-start(f32[816]{0:T(1024)S(1)} %fusion.615) | copy-start | bytes 9796
  580.5 61.2 %copy-start.154 = (f32[816,2048]{1,0:T(8,128)}, f32[816,2048]{1,0:T(8,128)S(1)}, u32[]{:S(2)}) copy-start(f32[816,2048]{1,0:T(8,128)S(1)} %fusion.625) | copy-start | bytes 20054020
  580.5 61.2 %copy-start.147 = (f32[1,512]{1,0:T(1,128)S(1)}, f32[1,512]{1,0:T(1,128)}, u32[]{:S(2)}) copy-start(f32[1,512]{1,0:T(1,128)} %get-tuple-element.679) | copy-start | bytes 6148
  580.5 61.2 %copy-start.148 = (bf16[2048,512]{1,0:T(8,128)(2,1)S(1)}, bf16[2048,512]{1,0:T(8,128)(2,1)}, u32[]{:S(2)}) copy-start(bf16[2048,512]{1,0:T(8,128)(2,1)} %param.36) | copy-start | bytes 6291460
  698.2 22.8 copy-start.47
  698.3 22.8 copy-start.72
  698.3 22.8 copy-start.76
  743.1 27.7 %copy-start.55 = (bf16[2,68,512]{2,1,0:T(8,128)(2,1)}, bf16[2,68,512]{2,1,0:T(8,128)(2,1)S(1)}, u32[]{:S(2)}) copy-start(bf16[2,68,512]{2,1,0:T(8,128)(2,1)S(1)} %get-tuple-element.758) | copy-start | bytes 417796 | tf_op jit(solution)/shard_map/cond
  805.2 560.4 %reduce-scatter.6.cloned.1.call-start = ((), (), s32[]{:S(2)}) async-start(), calls=%async_computation.12 | async-start | bytes 2506752 | tf_op jit(solution)/shard_map/reduce_scatter | solution.py:313
  810.4 37.9 %copy-start.50 = (f32[2,68,512]{2,1,0:T(8,128)S(1)}, f32[2,68,512]{2,1,0:T(8,128)}, u32[]{:S(2)}) copy-start(f32[2,68,512]{2,1,0:T(8,128)} %get-tuple-element.377) | copy-start | bytes 835588
  810.4 37.9 %copy-start.78 = (f32[2,68,512]{2,1,0:T(8,128)S(1)}, f32[2,68,512]{2,1,0:T(8,128)}, u32[]{:S(2)}) copy-start(f32[2,68,512]{2,1,0:T(8,128)} %copy-done.77) | copy-start | bytes 835588
  878.2 27.7 %copy-start.59 = (bf16[2,68,512]{2,1,0:T(8,128)(2,1)}, bf16[2,68,512]{2,1,0:T(8,128)(2,1)S(1)}, u32[]{:S(2)}) copy-start(bf16[2,68,512]{2,1,0:T(8,128)(2,1)S(1)} %get-tuple-element.770) | copy-start | bytes 417796 | tf_op jit(solution)/shard_map/cond
  940.4 425.3 %reduce-scatter.10.cloned.1.call-start = ((), (), s32[]{:S(2)}) async-start(), calls=%async_computation.14 | async-start | bytes 2506752 | tf_op jit(solution)/shard_map/reduce_scatter | solution.py:313
  945.6 38.7 %copy-start.45 = (f32[2,68,512]{2,1,0:T(8,128)S(1)}, f32[2,68,512]{2,1,0:T(8,128)}, u32[]{:S(2)}) copy-start(f32[2,68,512]{2,1,0:T(8,128)} %get-tuple-element.387) | copy-start | bytes 835588
  945.6 38.7 %copy-start.74 = (f32[2,68,512]{2,1,0:T(8,128)S(1)}, f32[2,68,512]{2,1,0:T(8,128)}, u32[]{:S(2)}) copy-start(f32[2,68,512]{2,1,0:T(8,128)} %copy-done.73) | copy-start | bytes 835588
  1014.3 27.7 %copy-start.61 = (bf16[2,68,512]{2,1,0:T(8,128)(2,1)}, bf16[2,68,512]{2,1,0:T(8,128)(2,1)S(1)}, u32[]{:S(2)}) copy-start(bf16[2,68,512]{2,1,0:T(8,128)(2,1)S(1)} %get-tuple-element.746) | copy-start | bytes 417796 | tf_op jit(solution)/shard_map/cond
  1077.0 547.7 %reduce-scatter.14.cloned.1.call-start = ((), (), s32[]{:S(2)}) async-start(), calls=%async_computation.16 | async-start | bytes 51249152 | tf_op jit(solution)/shard_map/reduce_scatter | solution.py:337
  1173.6 905.4 %reduce-scatter.12.cloned.1.call-start = ((), (), s32[]{:S(2)}) async-start(), calls=%async_computation.15 | async-start | bytes 51249152 | tf_op jit(solution)/shard_map/reduce_scatter | solution.py:337
  1288.5 1000.4 %all-reduce.32.cloned.1.call-start = ((), (), s32[]{:S(2)}) async-start(), calls=%async_computation.17 | async-start | bytes 20971520 | tf_op jit(solution)/shard_map/psum | solution.py:339
  (134 other events, 592.9 us)
Sparse Core Ops, SparseCore 0:
  9.6 239.8 all-gather.1
  805.4 41.6 reduce-scatter.7
  940.5 42.9 reduce-scatter.5
  1077.1 27.1 reduce-scatter.9
  1173.7 450.9 reduce-scatter.13
  1629.5 449.4 reduce-scatter.11
  2086.2 202.6 all-reduce.31
